TPU v7x, 256 devices: a whole 4x4x8 slice. The times are simulated.
256 devices in a mesh: seq: 64 (over y, z, core), head: 4 (over x).
Axes of the slice: x: 4, y: 4, z: 8, core: 2. Of those that a mesh axis runs over, the one named last changes fastest.
Arguments:
- queries: bfloat16 [65536, 4, 512], P(('seq', 'head')), may hold values from -12 to 12
- key_value: bfloat16 [65536, 4, 256], P(('seq', 'head')), may hold values from -5 to 5
- rand_blocks: int32 [256, 16, 3], replicated, may hold values from 0 to 255, as said below
Outputs:
- attended: bfloat16 [65536, 4, 512], P('seq', 'head')
Inputs may be any that keep to these rules, and one draw needn't show every extreme that they name: Block c is held by index c // 4 of seq. For each key-value head a and each aligned run of 4 query blocks, the 48 entries rand_blocks[c, a * 4 + g, :] of those blocks name blocks of any one holder at most 1 times, counted with repeats, and some holder exactly 1 times.
All inputs are finite; a program needn't handle non-finite values.
Results may differ from a plain program's by a relative error of at most 0.0039.
Values may be sent and summed in bfloat16 or wider, within the bound.
A program may use at most 192 MiB of HBM per device.

v0:
```python
import jax
import jax.numpy as jnp
import numpy as np
from jax import lax
from jax.sharding import PartitionSpec as P

HD = 128
BLOCK = 256


def partner(x, axis, apart):
    return lax.ppermute(x, axis, [(i, i ^ 1 << apart) for i in range(lax.axis_size(axis))])


def on_device(queries, key_value, rand_blocks):
    queries_here, pairs_here = (
        lax.all_to_all(queries, "head", split_axis=1, concat_axis=0, tiled=True),
        lax.all_to_all(key_value, "head", split_axis=1, concat_axis=0, tiled=True),
    )
    tokens_here = queries_here.shape[0]
    blocks_here = tokens_here // BLOCK
    heads_kv = pairs_here.shape[1]
    group_size = queries_here.shape[2] // HD
    query_blocks = queries_here.reshape(blocks_here, BLOCK, heads_kv, group_size, HD)
    pair_blocks = pairs_here.reshape(blocks_here, BLOCK, heads_kv, 2 * HD)
    score_scale = HD ** (-0.5)

    def finish_term(scores, values, form):
        block_max = jnp.max(scores, axis=-1)
        weights = jnp.exp(scores - block_max[..., None]).astype(jnp.bfloat16)
        totals = jnp.sum(weights, axis=-1, dtype=jnp.float32)
        partial_value = jnp.einsum(form, weights, values, preferred_element_type=jnp.float32)
        return (block_max, totals, partial_value)

    def combine(running, term):
        if running is None:
            return term
        highest = jnp.maximum(running[0], term[0])
        keep_old = jnp.exp(running[0] - highest)
        keep_new = jnp.exp(term[0] - highest)
        return (
            highest,
            keep_old * running[1] + keep_new * term[1],
            keep_old[..., None] * running[2] + keep_new[..., None] * term[2],
        )

    local_sets = [pair_blocks]
    for level in range(blocks_here.bit_length() - 1):
        distance = 1 << level
        folded = pair_blocks.reshape(
            blocks_here // (2 * distance), 2, distance, BLOCK, heads_kv, 2 * HD
        )
        local_sets.append(jnp.flip(folded, axis=1).reshape(pair_blocks.shape))
    seq_count = lax.axis_size("seq")
    my_index = lax.axis_index("seq")
    head_start = lax.axis_index("head") * heads_kv
    slot_count = blocks_here * group_size * 3
    capacity = -(-slot_count // seq_count)
    total_heads = rand_blocks.shape[1] // group_size
    all_requests = rand_blocks.reshape(seq_count, blocks_here, total_heads, group_size, 3)
    own_requests = lax.dynamic_slice_in_dim(all_requests, head_start, heads_kv, 2)
    requests = own_requests.transpose(0, 2, 1, 3, 4).reshape(seq_count, heads_kv, slot_count)
    holder = requests // blocks_here
    within = requests % blocks_here
    columns = np.arange(slot_count) % 3
    head_pick = jnp.arange(heads_kv, dtype=jnp.int32)[None, :, None]
    random_sets = []
    for column_index in range(3):
        active = columns == column_index
        earlier = np.tril(np.ones((slot_count, slot_count), dtype=bool), -1) & active[None, :]
        same_holder = holder[:, :, :, None] == holder[:, :, None, :]
        slot_rank = jnp.sum(same_holder & earlier[None, None], axis=-1, dtype=jnp.int32)
        is_mine = (holder == my_index) & active[None, None, :]
        matches = is_mine[:, :, None, :] & (
            slot_rank[:, :, None, :] == jnp.arange(capacity, dtype=jnp.int32)[None, None, :, None]
        )
        local_id = jnp.sum(jnp.where(matches, within[:, :, None, :], 0), axis=-1, dtype=jnp.int32)
        outgoing = pair_blocks[local_id, :, head_pick].reshape(
            seq_count * heads_kv * capacity, BLOCK, 2 * HD
        )
        own_holder = lax.dynamic_index_in_dim(holder, my_index, 0, keepdims=False)
        own_rank = lax.dynamic_index_in_dim(slot_rank, my_index, 0, keepdims=False)
        head_offset = jnp.arange(heads_kv, dtype=jnp.int32)[:, None] * capacity
        outgoing, positions = (
            outgoing,
            own_holder * (heads_kv * capacity) + head_offset + own_rank,
        )
        incoming = lax.all_to_all(outgoing, "seq", split_axis=0, concat_axis=0, tiled=True)
        picked = incoming[positions[:, column_index::3]]
        random_sets.append(picked.reshape(heads_kv, blocks_here, group_size, BLOCK, 2 * HD))

    def partner_shard(level):
        return partner(pairs_here, "seq", level).reshape(pair_blocks.shape)

    seq_levels = seq_count.bit_length() - 1
    running = None
    shards = [partner_shard(level) for level in range(seq_levels)]
    for chosen in local_sets + shards:
        shared_scores = (
            jnp.einsum(
                "bqkgd,bukd->bqkgu",
                query_blocks,
                chosen[..., :HD],
                preferred_element_type=jnp.float32,
            )
            * score_scale
        )
        running = combine(
            running, finish_term(shared_scores, chosen[..., HD:], "bqkgu,bukd->bqkgd")
        )
    for chosen in random_sets:
        random_scores = (
            jnp.einsum(
                "bqkgd,kbgud->bqkgu",
                query_blocks,
                chosen[..., :HD],
                preferred_element_type=jnp.float32,
            )
            * score_scale
        )
        running = combine(
            running, finish_term(random_scores, chosen[..., HD:], "bqkgu,kbgud->bqkgd")
        )
    attended = running[2] / running[1][..., None]
    return attended.astype(jnp.bfloat16).reshape(tokens_here, heads_kv, group_size * HD)


def solution(mesh):
    in_specs = (P(("seq", "head"), None, None), P(("seq", "head"), None, None), P())
    out_specs = P("seq", "head", None)
    return jax.shard_map(
        on_device, mesh=mesh, in_specs=in_specs, out_specs=out_specs, check_vma=False
    )
```

profile of v0, /device:TPU:1, one launch (start us, length us, event | category | flops | bytes accessed | tf_op | source)
XLA Modules:
  0.0 729.0 jit_solution(4346606090651757667)
XLA Ops:
  0.0 1.9 copy.116
  2.0 5.0 all-to-all-start
  6.9 2.4 copy.117
  9.3 1.6 reshape.1583
  12.2 1.4 convert_reduce_fusion.14
  14.4 3.5 all-to-all-start.1
  18.8 1.5 select_reduce_fusion.2
  20.3 5.4 gather_fusion.2
  25.7 4.1 all-to-all-done.1
  29.9 16.8 %all-to-all-start.3 = ((bf16[64,256,256]{2,1,0:T(8,128)(2,1)}), bf16[64,256,256]{2,1,0:T(8,128)(2,1)}, u32[]{:S(2)}, u32[]{:S(2)}) async-start(bf16[64,256,256]{2,1,0:T(8,128)(2,1)} %gather_fusion.2), calls=%async_computation.3 | async-start | bytes 16777216 | tf_op jit(solution)/shard_map/all_to_all | solution.py:88
  46.7 5.3 gather_fusion.4
  52.0 180.4 %all-to-all-done.3 = bf16[64,256,256]{2,1,0:T(8,128)(2,1)} async-done(((bf16[64,256,256]{2,1,0:T(8,128)(2,1)}), bf16[64,256,256]{2,1,0:T(8,128)(2,1)}, u32[]{:S(2)}, u32[]{:S(2)}) %all-to-all-start.3) | async-done | bytes 8388640 | tf_op jit(solution)/shard_map/all_to_all | solution.py:88
  232.4 6.0 all-to-all-start.4
  238.4 5.3 gather_fusion
  243.7 180.4 %all-to-all-done.4 = bf16[64,256,256]{2,1,0:T(8,128)(2,1)} async-done(((bf16[64,256,256]{2,1,0:T(8,128)(2,1)}), bf16[64,256,256]{2,1,0:T(8,128)(2,1)}, u32[]{:S(2)}, u32[]{:S(2)}) %all-to-all-start.4) | async-done | bytes 8388640 | tf_op jit(solution)/shard_map/all_to_all | solution.py:88
  424.1 6.0 all-to-all-start.2
  431.1 3.0 collective-permute-start.5
  434.5 5.1 collective-permute-start.3
  442.3 2.5 fusion.68
  444.8 2.5 fusion.70
  447.3 1.6 convert_reduce_fusion.10
  449.6 2.5 fusion.66
  452.1 16.3 %collective-permute-done.5 = bf16[1024,1,256]{2,0,1:T(8,128)(2,1)} collective-permute-done((bf16[1024,1,256]{2,0,1:T(8,128)(2,1)S(1)}, bf16[1024,1,256]{2,0,1:T(8,128)(2,1)}, u32[]{:S(2)}, u32[]{:S(2)}) %collective-permute-start.5) | collective-permute-done | bytes 524320 | tf_op jit(solution)/shard_map/ppermute | solution.py:12
  468.3 3.3 collective-permute-start
  471.7 3.7 bitcast_reduce_fusion.3
  475.4 18.3 %collective-permute-done.4 = bf16[1024,1,256]{2,0,1:T(8,128)(2,1)S(1)} collective-permute-done((bf16[1024,1,256]{2,0,1:T(8,128)(2,1)S(1)}, bf16[1024,1,256]{2,0,1:T(8,128)(2,1)S(1)}, u32[]{:S(2)}, u32[]{:S(2)}) %collective-permute-start.4) | collective-permute-done | bytes 524320 | tf_op jit(solution)/shard_map/ppermute | solution.py:12
  494.4 134.2 %collective-permute-done.3 = bf16[1024,1,256]{2,0,1:T(8,128)(2,1)} collective-permute-done((bf16[1024,1,256]{2,0,1:T(8,128)(2,1)S(1)}, bf16[1024,1,256]{2,0,1:T(8,128)(2,1)}, u32[]{:S(2)}, u32[]{:S(2)}) %collective-permute-start.3) | collective-permute-done | bytes 524320 | tf_op jit(solution)/shard_map/ppermute | solution.py:12
  628.6 1.7 bitcast_reduce_fusion.5
  630.2 27.3 %collective-permute-done.2 = bf16[1024,1,256]{2,0,1:T(8,128)(2,1)} collective-permute-done((bf16[1024,1,256]{2,0,1:T(8,128)(2,1)S(1)}, bf16[1024,1,256]{2,0,1:T(8,128)(2,1)}, u32[]{:S(2)}, u32[]{:S(2)}) %collective-permute-start.2) | collective-permute-done | bytes 524320 | tf_op jit(solution)/shard_map/ppermute | solution.py:12
  657.5 1.7 bitcast_reduce_fusion.6
  659.1 1.7 bitcast_reduce_fusion.7
  661.5 2.5 fusion.56
  664.0 3.5 fusion.58
  667.4 3.4 fusion.60
  670.8 3.4 fusion.62
  674.2 2.5 fusion.64
  676.8 1.6 convert_reduce_fusion.4
  678.4 1.8 convert_reduce_fusion.6
  680.2 1.6 convert_reduce_fusion.8
  681.9 4.1 gather_fusion.3
  685.9 5.4 gather_fusion.5
  694.4 2.3 fusion.50
  696.7 2.4 fusion.48
  699.1 4.1 gather_fusion.1
  704.9 1.5 copy-done
  706.4 1.6 convert_reduce_fusion.2
  711.0 15.5 %fusion.26 = bf16[4,256,1,4,128]{4,1,3,0,2:T(8,128)(2,1)S(1)} fusion(f32[4,4,128,256]{2,3,1,0:T(8,128)} %fusion.48, f32[4,4,128,256]{2,3,1,0:T(8,128)S(1)} %copy-done.10, f32[4,4,128,256]{2,3,1,0:T(8,128)S(1)} %fusion.52, f32[4,256,4,128]{3,1,2,0:T(8,128)S(1)} %copy-done.5, f32[4,256,4,128]{3,1,2,0:T(8,128)S(1)} %copy-done.6, ...), kind=kOutput, calls=%fused_computation.69 | convolution fusion | flops 289931264 | bytes 28966912 | tf_op jit(solution)/shard_map/bqkgu,bukd->bqkgd/dot_general | solution.py:32
  727.4 1.2 reshape.1617
  (93 shorter events, 17.6 us)
Async XLA Ops:
  0.0 12.1 %copy-start.12 = (pred[48,48]{1,0:T(8,128)(4,1)S(1)}, pred[48,48]{1,0:T(8,128)(4,1)}, u32[]{:S(2)}) copy-start(pred[48,48]{1,0:T(8,128)(4,1)} %constant.94) | copy-start | bytes 6916
  0.0 12.1 %copy-start.13 = (pred[48,48]{1,0:T(8,128)(4,1)S(1)}, pred[48,48]{1,0:T(8,128)(4,1)}, u32[]{:S(2)}) copy-start(pred[48,48]{1,0:T(8,128)(4,1)} %constant.92) | copy-start | bytes 6916
  0.0 12.1 %copy-start.14 = (pred[48,48]{1,0:T(8,128)(4,1)S(1)}, pred[48,48]{1,0:T(8,128)(4,1)}, u32[]{:S(2)}) copy-start(pred[48,48]{1,0:T(8,128)(4,1)} %constant.90) | copy-start | bytes 6916
  0.0 9.3 %copy-start.11 = (s32[256,16,3]{0,1,2:T(8,128)S(1)}, s32[256,16,3]{0,1,2:T(8,128)}, u32[]{:S(2)}) copy-start(s32[256,16,3]{0,1,2:T(8,128)} %param.11) | copy-start | bytes 147460
  1.9 16.9 %copy-start.15 = (pred[4,4,3]{0,1,2:T(4,128)(4,1)S(1)}, pred[4,4,3]{0,1,2:T(4,128)(4,1)}, u32[]{:S(2)}) copy-start(pred[4,4,3]{0,1,2:T(4,128)(4,1)} %constant.93) | copy-start | bytes 148
  1.9 16.9 %copy-start.16 = (pred[4,4,3]{0,1,2:T(4,128)(4,1)S(1)}, pred[4,4,3]{0,1,2:T(4,128)(4,1)}, u32[]{:S(2)}) copy-start(pred[4,4,3]{0,1,2:T(4,128)(4,1)} %constant.91) | copy-start | bytes 148
  1.9 16.9 %copy-start.17 = (pred[4,4,3]{0,1,2:T(4,128)(4,1)S(1)}, pred[4,4,3]{0,1,2:T(4,128)(4,1)}, u32[]{:S(2)}) copy-start(pred[4,4,3]{0,1,2:T(4,128)(4,1)} %constant.89) | copy-start | bytes 148
  2.0 12.5 %all-to-all-start = ((bf16[256,4,256]{2,0,1:T(8,128)(2,1)}), bf16[256,4,256]{2,0,1:T(8,128)(2,1)S(1)}, u32[]{:S(2)}, u32[]{:S(2)}) async-start(bf16[256,4,256]{2,0,1:T(8,128)(2,1)} %copy.116), calls=%async_computation | async-start | bytes 1048576 | tf_op jit(solution)/shard_map/all_to_all | solution.py:18
  14.4 15.5 %all-to-all-start.1 = ((bf16[256,4,512]{0,2,1:T(8,128)(2,1)}), bf16[256,4,512]{0,2,1:T(8,128)(2,1)S(1)}, u32[]{:S(2)}, u32[]{:S(2)}) async-start(bf16[256,4,512]{0,2,1:T(8,128)(2,1)} %copy.117), calls=%async_computation.1 | async-start | bytes 2097152 | tf_op jit(solution)/shard_map/all_to_all | solution.py:17
  29.9 202.5 %all-to-all-start.3 = ((bf16[64,256,256]{2,1,0:T(8,128)(2,1)}), bf16[64,256,256]{2,1,0:T(8,128)(2,1)}, u32[]{:S(2)}, u32[]{:S(2)}) async-start(bf16[64,256,256]{2,1,0:T(8,128)(2,1)} %gather_fusion.2), calls=%async_computation.3 | async-start | bytes 16777216 | tf_op jit(solution)/shard_map/all_to_all | solution.py:88
  232.4 191.7 %all-to-all-start.4 = ((bf16[64,256,256]{2,1,0:T(8,128)(2,1)}), bf16[64,256,256]{2,1,0:T(8,128)(2,1)}, u32[]{:S(2)}, u32[]{:S(2)}) async-start(bf16[64,256,256]{2,1,0:T(8,128)(2,1)} %gather_fusion.4), calls=%async_computation.4 | async-start | bytes 16777216 | tf_op jit(solution)/shard_map/all_to_all | solution.py:88
  424.1 275.0 %all-to-all-start.2 = ((bf16[64,256,256]{2,1,0:T(8,128)(2,1)}), bf16[64,256,256]{2,1,0:T(8,128)(2,1)}, u32[]{:S(2)}, u32[]{:S(2)}) async-start(bf16[64,256,256]{2,1,0:T(8,128)(2,1)} %gather_fusion), calls=%async_computation.2 | async-start | bytes 16777216 | tf_op jit(solution)/shard_map/all_to_all | solution.py:88
  431.1 37.3 %collective-permute-start.5 = (bf16[1024,1,256]{2,0,1:T(8,128)(2,1)S(1)}, bf16[1024,1,256]{2,0,1:T(8,128)(2,1)}, u32[]{:S(2)}, u32[]{:S(2)}) collective-permute-start(bf16[1024,1,256]{2,0,1:T(8,128)(2,1)S(1)} %bitcast.658), channel_id=1, source_target_pairs={{0,128},{4,132},{8,136},{12,140},{16,144},{20,148},{24,152},{28,15... | collective-permute-start | bytes 1572872 | tf_op jit(solution)/shard_map/ppermute | solution.py:12
  434.1 59.5 %collective-permute-start.4 = (bf16[1024,1,256]{2,0,1:T(8,128)(2,1)S(1)}, bf16[1024,1,256]{2,0,1:T(8,128)(2,1)S(1)}, u32[]{:S(2)}, u32[]{:S(2)}) collective-permute-start(bf16[1024,1,256]{2,0,1:T(8,128)(2,1)S(1)} %bitcast.659), channel_id=1, source_target_pairs={{0,64},{4,68},{8,72},{12,76},{16,80},{20,84},{24,88},{28,92},{32,9... | collective-permute-start | bytes 1572872 | tf_op jit(solution)/shard_map/ppermute | solution.py:12
  434.5 194.0 %collective-permute-start.3 = (bf16[1024,1,256]{2,0,1:T(8,128)(2,1)S(1)}, bf16[1024,1,256]{2,0,1:T(8,128)(2,1)}, u32[]{:S(2)}, u32[]{:S(2)}) collective-permute-start(bf16[1024,1,256]{2,0,1:T(8,128)(2,1)S(1)} %bitcast.660), channel_id=1, source_target_pairs={{0,32},{4,36},{8,40},{12,44},{16,48},{20,52},{24,56},{28,60},{32,0... | collective-permute-start | bytes 1572872 | tf_op jit(solution)/shard_map/ppermute | solution.py:12
  439.7 217.8 %collective-permute-start.2 = (bf16[1024,1,256]{2,0,1:T(8,128)(2,1)S(1)}, bf16[1024,1,256]{2,0,1:T(8,128)(2,1)}, u32[]{:S(2)}, u32[]{:S(2)}) collective-permute-start(bf16[1024,1,256]{2,0,1:T(8,128)(2,1)S(1)} %bitcast.661), channel_id=1, source_target_pairs={{0,16},{4,20},{8,24},{12,28},{16,0},{20,4},{24,8},{28,12},{32,48},... | collective-permute-start | bytes 1572872 | tf_op jit(solution)/shard_map/ppermute | solution.py:12
  440.5 218.6 %collective-permute-start.1 = (bf16[1024,1,256]{2,0,1:T(8,128)(2,1)S(1)}, bf16[1024,1,256]{2,0,1:T(8,128)(2,1)}, u32[]{:S(2)}, u32[]{:S(2)}) collective-permute-start(bf16[1024,1,256]{2,0,1:T(8,128)(2,1)S(1)} %bitcast.662), channel_id=1, source_target_pairs={{0,8},{4,12},{8,0},{12,4},{16,24},{20,28},{24,16},{28,20},{32,40},... | collective-permute-start | bytes 1572872 | tf_op jit(solution)/shard_map/ppermute | solution.py:12
  468.3 192.4 %collective-permute-start = (bf16[1024,1,256]{2,0,1:T(8,128)(2,1)S(1)}, bf16[1024,1,256]{2,0,1:T(8,128)(2,1)S(1)}, u32[]{:S(2)}, u32[]{:S(2)}) collective-permute-start(bf16[1024,1,256]{2,0,1:T(8,128)(2,1)S(1)} %bitcast.667), channel_id=1, source_target_pairs={{0,4},{4,0},{8,12},{12,8},{16,20},{20,16},{24,28},{28,24},{32,36},... | collective-permute-start | bytes 1572872 | tf_op jit(solution)/shard_map/ppermute | solution.py:12
  691.3 1.6 copy-start.1
  703.1 5.1 copy-start.8
  703.1 5.1 copy-start.9
  703.2 5.1 copy-start.10
  703.9 2.6 copy-start
  703.9 4.4 copy-start.6
  703.9 4.7 copy-start.7
  706.4 2.8 copy-start.2
  706.4 3.4 copy-start.3
  706.4 4.0 copy-start.4
  706.4 4.6 copy-start.5
where the time goes:
time: 738 us; the launch traced here: 729 us
  waiting for transfers between devices  562 us (76%)
  matrix products  58.3 us (8%)
  starting transfers between devices  50.2 us (7%)
  local copies, waits for them, and re-layouts  43.4 us (6%)
  other arithmetic  14.6 us (2%)
    all_to_all x3, waiting for transfers between devices, on_device(): lax.all_to_all(outgoing, 'seq', split_axis=0, concat_axis=0, tiled=True)  361 us
    ppermute x6, waiting for transfers between devices, partner(): lax.ppermute(x, axis, [(i, i ^ 1 << apart) for i in range(lax.axis_size(a...  196 us
    dot_general x12, matrix products, finish_term(): jnp.einsum(form, weights, values, preferred_element_type=jnp.float32)  43.9 us
    all_to_all x3, starting transfers between devices, on_device(): lax.all_to_all(outgoing, 'seq', split_axis=0, concat_axis=0, tiled=True)  28.7 us
    gather x3, local copies, waits for them, and re-layouts, on_device(): pair_blocks[local_id, :, head_pick]  16.1 us
  transfers between devices with their start and end apart: 11, of which 8 were waited for; matrix products, arithmetic and copies ran while one was open for 12% of the time, Pallas kernels for 0%

commit v1 on v0

v1 whole, which is shorter than its diff:
```python
import jax
import jax.numpy as jnp
import numpy as np
from jax import lax
from jax.experimental import pallas as pl
from jax.experimental.pallas import tpu as pltpu
from jax.sharding import PartitionSpec as P

HD = 128
BLOCK = 256
LISTED = 21
SHARED = 9


def attend_kernel(table, q_ref, kv_ref, o_ref, kbuf, vbuf, sem):
    c = pl.program_id(0)
    slot = c % 2

    def copies(step, where):
        made = []
        for j in range(LISTED):
            block = table[step * LISTED + j]
            made.append(pltpu.make_async_copy(
                kv_ref.at[block, :, 0:HD], kbuf.at[where, pl.ds(j * BLOCK, BLOCK)], sem.at[where, 0, j]))
            made.append(pltpu.make_async_copy(
                kv_ref.at[block, :, HD:2 * HD], vbuf.at[where, pl.ds(j * BLOCK, BLOCK), 0:HD], sem.at[where, 1, j]))
        return made

    @pl.when(c == 0)
    def _():
        for copy in copies(0, 0):
            copy.start()
        vbuf[:, :, HD:2 * HD] = jnp.ones((2, LISTED * BLOCK, HD), jnp.bfloat16)

    @pl.when(c + 1 < pl.num_programs(0))
    def _():
        for copy in copies(c + 1, 1 - slot):
            copy.start()

    for copy in copies(c, slot):
        copy.wait()
    factor = HD ** (-0.5) * np.log2(np.e)
    for g in range(4):
        q = q_ref[:, g * HD:(g + 1) * HD]
        nt = (((1,), (1,)), ((), ()))
        lo = SHARED * BLOCK
        ro = (SHARED + 3 * g) * BLOCK
        s1 = lax.dot_general(q, kbuf[slot, 0:lo], nt, preferred_element_type=jnp.float32)
        s2 = lax.dot_general(q, kbuf[slot, ro:ro + 3 * BLOCK], nt, preferred_element_type=jnp.float32)
        m = jnp.maximum(jnp.max(s1, axis=-1, keepdims=True), jnp.max(s2, axis=-1, keepdims=True))
        p1 = jnp.exp2((s1 - m) * factor).astype(jnp.bfloat16)
        p2 = jnp.exp2((s2 - m) * factor).astype(jnp.bfloat16)
        o = jnp.dot(p1, vbuf[slot, 0:lo], preferred_element_type=jnp.float32)
        o += jnp.dot(p2, vbuf[slot, ro:ro + 3 * BLOCK], preferred_element_type=jnp.float32)
        o_ref[:, g * HD:(g + 1) * HD] = (o[:, :HD] / o[:, HD:]).astype(jnp.bfloat16)


def on_device(queries, key_value, rand_blocks):
    q = lax.all_to_all(queries, "head", split_axis=1, concat_axis=0, tiled=True).reshape(1024, 512)
    kv = lax.all_to_all(key_value, "head", split_axis=1, concat_axis=0, tiled=True).reshape(4, BLOCK, 2 * HD)
    seq = lax.axis_index("seq")
    head = lax.axis_index("head")
    kv_all = lax.all_gather(kv, "seq", axis=0, tiled=True)
    blocks = seq * 4 + jnp.arange(4, dtype=jnp.int32)
    flips = jnp.array([0] + [1 << i for i in range(8)], dtype=jnp.int32)
    shared = blocks[:, None] ^ flips[None]
    mine = lax.dynamic_slice(rand_blocks, (seq * 4, head * 4, 0), (4, 4, 3)).reshape(4, 12)
    table = jnp.concatenate([shared, mine], axis=1).reshape(-1).astype(jnp.int32)
    out = pl.pallas_call(
        attend_kernel,
        grid_spec=pltpu.PrefetchScalarGridSpec(
            num_scalar_prefetch=1, grid=(4,),
            in_specs=[pl.BlockSpec((BLOCK, 4 * HD), lambda c, t: (c, 0)),
                      pl.BlockSpec(memory_space=pl.ANY)],
            out_specs=pl.BlockSpec((BLOCK, 4 * HD), lambda c, t: (c, 0)),
            scratch_shapes=[pltpu.VMEM((2, LISTED * BLOCK, HD), jnp.bfloat16),
                            pltpu.VMEM((2, LISTED * BLOCK, 2 * HD), jnp.bfloat16),
                            pltpu.SemaphoreType.DMA((2, 2, LISTED))]),
        out_shape=jax.ShapeDtypeStruct((1024, 512), jnp.bfloat16),
        compiler_params=pltpu.CompilerParams(dimension_semantics=("arbitrary",), vmem_limit_bytes=60 << 20),
        name="attend",
    )(table, q, kv_all)
    return out.reshape(1024, 1, 512)


def solution(mesh):
    in_specs = (P(("seq", "head"), None, None), P(("seq", "head"), None, None), P())
    return jax.shard_map(on_device, mesh=mesh, in_specs=in_specs, out_specs=P("seq", "head", None), check_vma=False)
```

time: 738 us -> 196 us (0.27); the launches traced: 729 us -> 196 us
  waiting for transfers between devices: 562 us -> 138 us
  matrix products: 58.3 us -> 0 us
  starting transfers between devices: 50.2 us -> 3.52 us
  local copies, waits for them, and re-layouts: 43.4 us -> 4.44 us
  Pallas kernels: 0 us -> 23.7 us
  other arithmetic: 14.6 us -> 0.81 us
  blocking collectives: 0 us -> 12.6 us
  between operations: 0.89 us -> 13.4 us
    all_to_all x4 -> x0, waiting for transfers between devices: 362 us -> none  [the longest x3 361 us: on_device(): lax.all_to_all(outgoing, 'seq', split_axis=0, concat_axis=0, tiled=True)]
    ppermute x6 -> x0, waiting for transfers between devices: 196 us -> none  [partner(): lax.ppermute(x, axis, [(i, i ^ 1 << apart) for i in range(lax.axis_size(a...]
    all_gather x0 -> x1, waiting for transfers between devices: none -> 127 us  [on_device(): kv_all = lax.all_gather(kv, 'seq', axis=0, tiled=True)]
    dot_general x24 -> x0, matrix products: 58.3 us -> none  [the longest x12 43.9 us: finish_term(): jnp.einsum(form, weights, values, preferred_element_type=jnp.float32)]
    all_to_all x4 -> x0, starting transfers between devices: 33.7 us -> none  [the longest x3 28.7 us: on_device(): lax.all_to_all(outgoing, 'seq', split_axis=0, concat_axis=0, tiled=True)]
    gather x6 -> x0, local copies, waits for them, and re-layouts: 29.6 us -> none  [the longest x3 16.1 us: on_device(): pair_blocks[local_id, :, head_pick]]
    pallas_call x0 -> x1, Pallas kernels: none -> 23.7 us  [on_device(): pl.pallas_call(attend_kernel, grid_spec=pltpu.PrefetchScalarGridSpec(num_...]
    ppermute x6 -> x0, starting transfers between devices: 13 us -> none  [partner(): lax.ppermute(x, axis, [(i, i ^ 1 << apart) for i in range(lax.axis_size(a...]
  transfers between devices with their start and end apart: 11 -> 2, of which waited for: 8 -> 2; matrix products, arithmetic and copies ran while one was open for 12% -> 2% of each run, Pallas kernels for 0% -> 0%
where the time goes in v1:
time: 196 us
  waiting for transfers between devices  138 us (70%)
  Pallas kernels  23.7 us (12%)
  between operations  13.4 us (7%)
  blocking collectives  12.6 us (6%)
  local copies, waits for them, and re-layouts  4.44 us (2%)
  starting transfers between devices  3.52 us (2%)
    all_gather x1, waiting for transfers between devices, on_device(): kv_all = lax.all_gather(kv, 'seq', axis=0, tiled=True)  127 us
    pallas_call x1, Pallas kernels, on_device(): pl.pallas_call(attend_kernel, grid_spec=pltpu.PrefetchScalarGridSpec(num_...  23.7 us
    all_to_all x1, blocking collectives, on_device(): lax.all_to_all(key_value, 'head', split_axis=1, concat_axis=0, tiled=True)  12.6 us
    all_to_all x1, waiting for transfers between devices, on_device(): lax.all_to_all(queries, 'head', split_axis=1, concat_axis=0, tiled=True)  10.5 us
  transfers between devices with their start and end apart: 2, of which 2 were waited for; matrix products, arithmetic and copies ran while one was open for 2% of the time, Pallas kernels for 0%

profile of v1, /device:TPU:1, one launch (start us, length us, event | category | flops | bytes accessed | tf_op | source)
XLA Modules:
  0.0 196.2 jit_solution(9987631787084159116)
XLA Ops:
  6.5 0.0 copy-start
  6.5 0.0 all-gather.3.cloned.1.call-start
  6.5 1.1 copy.13
  7.7 12.6 %all_to_all.30 = bf16[256,4,256]{2,0,1:T(8,128)(2,1)} all-to-all(bf16[256,4,256]{2,0,1:T(8,128)(2,1)S(1)} %copy.13), channel_id=1, replica_groups=mesh['seq'=64,'head'=4] {'head'}, dimensions={1} | all-to-all | bytes 1048576 | tf_op jit(solution)/shard_map/all_to_all | solution.py:60
  20.2 0.0 all-gather.3.cloned.1.call-update
  20.3 2.4 %copy.12 = bf16[256,4,512]{2,0,1:T(8,128)(2,1)} copy(bf16[256,4,512]{2,1,0:T(4,128)(2,1)} %param.4) | data formatting | bytes 2097152 | tf_op args[0]
  22.7 3.5 %all-to-all-start = ((bf16[256,4,512]{2,0,1:T(8,128)(2,1)}), bf16[256,4,512]{2,0,1:T(8,128)(2,1)S(1)}, u32[]{:S(2)}, u32[]{:S(2)}) async-start(bf16[256,4,512]{2,0,1:T(8,128)(2,1)} %copy.12), calls=%async_computation | async-start | bytes 2097152 | tf_op jit(solution)/shard_map/all_to_all | solution.py:59
  26.2 0.0 copy-done
  26.2 0.1 constant_dynamic-slice_fusion
  26.3 0.1 copy.11
  26.4 0.1 reshape.22
  26.5 0.7 broadcast_xor_fusion
  27.2 0.1 pad_add_fusion
  27.3 0.6 reshape.23.table
  27.9 10.5 %all-to-all-done = bf16[256,4,512]{2,0,1:T(8,128)(2,1)S(1)} async-done(((bf16[256,4,512]{2,0,1:T(8,128)(2,1)}), bf16[256,4,512]{2,0,1:T(8,128)(2,1)S(1)}, u32[]{:S(2)}, u32[]{:S(2)}) %all-to-all-start) | async-done | bytes 1048608 | tf_op jit(solution)/shard_map/all_to_all | solution.py:59
  38.5 0.0 copy-start.1
  38.5 127.2 %all-gather.3.cloned.1.call-done = bf16[256,256,1,256]{3,1,2,0:T(8,128)(2,1)} async-done(((bf16[4,256,1,256]{3,1,2,0:T(8,128)(2,1)}), bf16[256,256,1,256]{3,1,2,0:T(8,128)(2,1)}) %all-gather.3.cloned.1.call-update) | async-done | bytes 33554448 | tf_op jit(solution)/shard_map/all_gather | solution.py:63
  165.6 0.0 copy-done.1
  165.6 23.7 %attend.1 = bf16[1024,512]{1,0:T(8,128)(2,1)} custom-call(s32[84]{0:T(128)} %reshape.23.table, bf16[1024,512]{1,0:T(8,128)(2,1)} %bitcast.11, bf16[256,256,256]{2,1,0:T(8,128)(2,1)} %bitcast.10), custom_call_target="tpu_custom_call" | custom-call | tf_op jit(solution)/shard_map/attend/pallas_call | solution.py:69
  (1 shorter events, 0.0 us)
Async XLA Ops:
  6.5 19.7 %copy-start = (s32[256,16,3]{0,1,2:T(8,128)S(1)}, s32[256,16,3]{0,1,2:T(8,128)}, u32[]{:S(2)}) copy-start(s32[256,16,3]{0,1,2:T(8,128)} %param.6) | copy-start | bytes 147460
  6.5 159.1 %all-gather.3.cloned.1.call-start = ((), (), s32[]{:S(2)}) async-start(), calls=%async_computation.2 | async-start | bytes 34078720 | tf_op jit(solution)/shard_map/all_gather | solution.py:63
  22.7 15.8 %all-to-all-start = ((bf16[256,4,512]{2,0,1:T(8,128)(2,1)}), bf16[256,4,512]{2,0,1:T(8,128)(2,1)S(1)}, u32[]{:S(2)}, u32[]{:S(2)}) async-start(bf16[256,4,512]{2,0,1:T(8,128)(2,1)} %copy.12), calls=%async_computation | async-start | bytes 2097152 | tf_op jit(solution)/shard_map/all_to_all | solution.py:59
  38.5 127.2 %copy-start.1 = (bf16[256,4,512]{2,0,1:T(8,128)(2,1)}, bf16[256,4,512]{2,0,1:T(8,128)(2,1)S(1)}, u32[]{:S(2)}) copy-start(bf16[256,4,512]{2,0,1:T(8,128)(2,1)S(1)} %all-to-all-done) | copy-start | bytes 3145732
Sparse Core Ops, SparseCore 0:
  20.4 145.1 all-gather.2

commit v2 on v1

--- a/solution.py
+++ b/solution.py
@@ -55,12 +55,212 @@
         o_ref[:, g * HD:(g + 1) * HD] = (o[:, :HD] / o[:, HD:]).astype(jnp.bfloat16)
 
 
+MESH = pl.DeviceIdType.MESH
+CUT = 104
+NY = 4
+NZ = 8
+
+
+def forward_rules():
+    rules = {}
+    todo = [("B", 0, 0, None), ("A", 0, 0, None)]
+    while todo:
+        piece = todo.pop(0)
+        if piece in rules:
+            continue
+        part, oy, oz, half = piece
+        sends = []
+
+        def go(axis, at, edge, way, name):
+            side = 0 if way > 0 else 1
+            if abs(at) < edge:
+                sends.append((axis, way, name(at - way, half)))
+            elif half is None or half == side:
+                sends.append((axis, way, name(edge + 1, side)))
+
+        def along_z(way):
+            go("z", oz, 3, way, lambda at, h: (part, oy, at, h))
+
+        def along_y(way):
+            go("y", oy, 1, way, lambda at, h: (part, at, oz, h))
+
+        first, first_at, first_edge, second, second_at = (
+            (along_y, oy, 2, along_z, oz) if part == "A" else (along_z, oz, 4, along_y, oy))
+        second_edge = 4 if part == "A" else 2
+        if second_at == 0:
+            if first_at == 0:
+                first(1), first(-1)
+            elif first_at != first_edge:
+                first(1 if first_at < 0 else -1)
+            second(1), second(-1)
+        elif second_at != second_edge:
+            second(1 if second_at < 0 else -1)
+        rules[piece] = sends
+        todo += [send[2] for send in sends]
+    return rules
+
+
+def arrival_order(rules):
+    size = {"A": CUT, "B": BLOCK - CUT}
+    free, order, count = {}, [], 2
+    events = [(0.0, 0, ("B", 0, 0, None)), (0.0, 1, ("A", 0, 0, None))]
+    while events:
+        events.sort()
+        now, _, piece = events.pop(0)
+        order.append(piece)
+        for axis, way, sent in rules[piece]:
+            rows = size[sent[0]] * (1.0 if sent[3] is None else 0.5)
+            done = max(now, free.get((axis, way), 0.0)) + rows
+            free[axis, way] = done
+            events.append((done + 38.0, count, sent))
+            count += 1
+    return order
+
+
+RULES = forward_rules()
+ORDER = arrival_order(RULES)
+FAR = [p for p in ORDER if p[1:3] != (0, 0)]
+SLOT = {p: i for i, p in enumerate(FAR)}
+NEAR = {("y", 1): 0, ("y", -1): 1, ("z", 1): 2, ("z", -1): 3}
+FIRST = [("z", 1, "B"), ("z", -1, "B"), ("y", 1, "A"), ("y", -1, "A"), ("z", 1, "A"), ("z", -1, "A"), ("y", 1, "B"), ("y", -1, "B")]
+
+
+def gather_kernel(kvh, qh, kv, q, send, recv, send_core, recv_core, send1, recv1, send_own, recv_own, sendx, recvx, local):
+    seq = lax.axis_index("seq")
+    x = lax.axis_index("head")
+    core = lax.rem(seq, 2)
+    z = lax.rem(seq // 2, NZ)
+    y = seq // (2 * NZ)
+
+    def at(oy, oz, c):
+        return (lax.rem(y + (oy + NY), NY) * NZ + lax.rem(z + (oz + NZ), NZ)) * 2 + c
+
+    where = {("y", 1): at(1, 0, core), ("y", -1): at(-1, 0, core), ("z", 1): at(0, 1, core), ("z", -1): at(0, -1, core)}
+    sibling = at(0, 0, 1 - core)
+    barrier = pltpu.get_barrier_semaphore()
+    for target in list(where.values()) + [sibling]:
+        pl.semaphore_signal(barrier, inc=1, device_id={"seq": target, "head": x}, device_id_type=MESH)
+    for r in (1, 2, 3):
+        pl.semaphore_signal(barrier, inc=1, device_id={"seq": seq, "head": lax.rem(x + r, 4)}, device_id_type=MESH)
+    own_kv = pltpu.make_async_copy(kvh.at[x], kv.at[seq * 4 + x], local.at[0])
+    own_q = pltpu.make_async_copy(qh.at[x], q.at[x], local.at[1])
+    own_kv.start()
+    own_q.start()
+    pl.semaphore_wait(barrier, 8)
+
+    def remote(src, dst, s, r, target, head):
+        return pltpu.make_async_remote_copy(src_ref=src, dst_ref=dst, send_sem=s, recv_sem=r,
+                                            device_id={"seq": target, "head": head}, device_id_type=MESH)
+
+    everything = []
+
+    def x_copy(source, target, which, r):
+        to = lax.rem(x + r, 4)
+        return remote(source.at[to], target, sendx.at[which, r], recvx.at[which, r], seq, to)
+
+    kv_x = {r: x_copy(kvh, kv.at[seq * 4 + x], 0, r) for r in (1, 3, 2)}
+    q_x = {r: x_copy(qh, q.at[x], 1, r) for r in (1, 3, 2)}
+    for r in (1, 3, 2):
+        kv_x[r].start()
+
+    def rows(part):
+        return pl.ds(0, CUT) if part == "A" else pl.ds(CUT, BLOCK - CUT)
+
+    def first_copy(axis, way, part, r):
+        block = kv.at[seq * 4 + lax.rem(x + 4 - r, 4), rows(part)]
+        i = NEAR[axis, way]
+        p = 0 if part == "A" else 1
+        return remote(block, block, send1.at[i, p, r], recv1.at[i, p, r], where[axis, way], x)
+
+    def own_copy(r):
+        block = kv.at[seq * 4 + lax.rem(x + 4 - r, 4)]
+        return remote(block, block, send_own.at[r], recv_own.at[r], sibling, x)
+
+    def piece_ref(piece, c):
+        part, oy, oz, half = piece
+        start, count = (0, 4) if half is None else (2 * half, 2)
+        return kv.at[pl.ds(at(oy, oz, c) * 4 + start, count), rows(part)]
+
+    def far_copy(held, axis, way, sent):
+        part, oy, oz, half = sent
+        mine = (part, held[1], held[2], half)
+        ref = piece_ref(mine, core)
+        i = SLOT[sent]
+        return remote(ref, ref, send.at[i], recv.at[i], where[axis, way], x)
+
+    def core_copy(piece):
+        ref = piece_ref(piece, core)
+        i = SLOT[piece]
+        return remote(ref, ref, send_core.at[i], recv_core.at[i], sibling, x)
+
+    for r in (0, 1, 3, 2):
+        if r == 0:
+            own_kv.wait()
+        else:
+            kv_x[r].wait_recv()
+        for axis, way, part in FIRST:
+            copy = first_copy(axis, way, part, r)
+            copy.start()
+            everything.append(copy)
+        copy = own_copy(r)
+        copy.start()
+        everything.append(copy)
+        if r == 0:
+            for k in (1, 3, 2):
+                q_x[k].start()
+
+    for piece in FAR:
+        part, oy, oz, half = piece
+        if half is None and abs(oy) + abs(oz) == 1:
+            axis, way = ("y", -oy) if oy else ("z", -oz)
+            for r in (0, 1, 3, 2):
+                first_copy(axis, way, part, r).wait_recv()
+        else:
+            ref = piece_ref(piece, core)
+            i = SLOT[piece]
+            remote(ref, ref, send.at[i], recv.at[i], sibling, x).wait_recv()
+        for axis, way, sent in RULES[piece]:
+            copy = far_copy(piece, axis, way, sent)
+            copy.start()
+            everything.append(copy)
+        copy = core_copy(piece)
+        copy.start()
+        everything.append(copy)
+
+    for r in (0, 1, 3, 2):
+        block = kv.at[seq * 4 + lax.rem(x + 4 - r, 4)]
+        remote(block, block, send_own.at[r], recv_own.at[r], sibling, x).wait_recv()
+    for piece in FAR:
+        core_copy(piece).wait_recv()
+    own_q.wait()
+    for r in (1, 3, 2):
+        q_x[r].wait_recv()
+        q_x[r].wait_send()
+        kv_x[r].wait_send()
+    for copy in everything:
+        copy.wait_send()
+
+
+def gather(kvh, qh):
+    dma = pltpu.SemaphoreType.DMA
+    n = len(FAR)
+    return pl.pallas_call(
+        gather_kernel,
+        out_shape=(jax.ShapeDtypeStruct((256, BLOCK, 2 * HD), jnp.bfloat16), jax.ShapeDtypeStruct((4, BLOCK, 4 * HD), jnp.bfloat16)),
+        in_specs=[pl.BlockSpec(memory_space=pltpu.VMEM)] * 2,
+        out_specs=[pl.BlockSpec(memory_space=pl.ANY)] * 2,
+        scratch_shapes=[dma((n,)), dma((n,)), dma((n,)), dma((n,)), dma((4, 2, 4)), dma((4, 2, 4)), dma((4,)), dma((4,)),
+                        dma((2, 4)), dma((2, 4)), dma((2,))],
+        compiler_params=pltpu.CompilerParams(collective_id=0, has_side_effects=True),
+        name="gather",
+    )(kvh, qh)
+
+
 def on_device(queries, key_value, rand_blocks):
-    q = lax.all_to_all(queries, "head", split_axis=1, concat_axis=0, tiled=True).reshape(1024, 512)
-    kv = lax.all_to_all(key_value, "head", split_axis=1, concat_axis=0, tiled=True).reshape(4, BLOCK, 2 * HD)
+    kv_all, q = gather(key_value.transpose(1, 0, 2), queries.transpose(1, 0, 2))
+    q = q.reshape(1024, 512)
     seq = lax.axis_index("seq")
     head = lax.axis_index("head")
-    kv_all = lax.all_gather(kv, "seq", axis=0, tiled=True)
     blocks = seq * 4 + jnp.arange(4, dtype=jnp.int32)
     flips = jnp.array([0] + [1 << i for i in range(8)], dtype=jnp.int32)
     shared = blocks[:, None] ^ flips[None]

time: 196 us -> 141 us (0.72)
  waiting for transfers between devices: 138 us -> 0 us
  Pallas kernels: 23.7 us -> 134 us
  between operations: 13.4 us -> 0.02 us
  blocking collectives: 12.6 us -> 0 us
  starting transfers between devices: 3.52 us -> 0 us
    all_gather x1 -> x0, waiting for transfers between devices: 127 us -> none  [on_device(): kv_all = lax.all_gather(kv, 'seq', axis=0, tiled=True)]
    pallas_call x0 -> x1, Pallas kernels: none -> 111 us  [gather(): pl.pallas_call(gather_kernel, out_shape=(jax.ShapeDtypeStruct((256, BLOCK...]
    all_to_all x1 -> x0, blocking collectives: 12.6 us -> none  [on_device(): lax.all_to_all(key_value, 'head', split_axis=1, concat_axis=0, tiled=True)]
    all_to_all x1 -> x0, waiting for transfers between devices: 10.5 us -> none  [on_device(): lax.all_to_all(queries, 'head', split_axis=1, concat_axis=0, tiled=True)]
    all_to_all x1 -> x0, starting transfers between devices: 3.52 us -> none  [on_device(): lax.all_to_all(queries, 'head', split_axis=1, concat_axis=0, tiled=True)]
    unnamed x6 -> x4, local copies, waits for them, and re-layouts: 3.53 us -> 4.35 us
  transfers between devices with their start and end apart: 2 -> 0, of which waited for: 2 -> 0; matrix products, arithmetic and copies ran while one was open for 2% -> 0% of each run, Pallas kernels for 0% -> 0%
where the time goes in v2:
time: 141 us; the launch traced here: 140 us
  Pallas kernels  134 us (95%)
  local copies, waits for them, and re-layouts  5.24 us (4%)
    pallas_call x1, Pallas kernels, gather(): pl.pallas_call(gather_kernel, out_shape=(jax.ShapeDtypeStruct((256, BLOCK...  111 us
    pallas_call x1, Pallas kernels, on_device(): pl.pallas_call(attend_kernel, grid_spec=pltpu.PrefetchScalarGridSpec(num_...  23.7 us
    unnamed x4, local copies, waits for them, and re-layouts  4.35 us

profile of v2, /device:TPU:1, one launch (start us, length us, event | category | flops | bytes accessed | tf_op | source)
XLA Modules:
  0.0 140.5 jit_solution(6031954580864679181)
XLA Ops:
  0.0 0.0 copy-start
  0.0 0.7 broadcast_xor_fusion
  0.7 0.1 copy-done
  0.8 0.1 constant_dynamic-slice_fusion
  0.9 0.1 copy.8
  1.0 0.1 reshape.17
  1.1 0.1 pad_add_fusion
  1.2 0.6 reshape.18.table
  1.8 1.9 %copy.14 = bf16[256,4,256]{2,0,1:T(8,128)(2,1)} copy(bf16[256,4,256]{2,1,0:T(4,128)(2,1)} %param.5) | data formatting | bytes 1048576 | tf_op args[1]
  3.7 2.4 %copy.13 = bf16[256,4,512]{2,0,1:T(8,128)(2,1)} copy(bf16[256,4,512]{2,1,0:T(4,128)(2,1)} %param.4) | data formatting | bytes 2097152 | tf_op args[0]
  6.1 110.7 %gather.1 = (bf16[256,256,256]{2,1,0:T(8,128)(2,1)}, bf16[4,256,512]{2,1,0:T(8,128)(2,1)}) custom-call(bf16[4,256,256]{2,1,0:T(8,128)(2,1)} %bitcast.9, bf16[4,256,512]{2,1,0:T(8,128)(2,1)} %bitcast.8), custom_call_target="tpu_custom_call" | custom-call | tf_op jit(solution)/shard_map/gather/pallas_call | solution.py:247
  116.8 23.7 %attend.1 = bf16[1024,512]{1,0:T(8,128)(2,1)} custom-call(s32[84]{0:T(128)} %reshape.18.table, bf16[1024,512]{1,0:T(8,128)(2,1)} %bitcast.10, bf16[256,256,256]{2,1,0:T(8,128)(2,1)} %get-tuple-element.8.kv_ref), custom_call_target="tpu_custom_call" | custom-call | tf_op jit(solution)/shard_map/attend/pallas_call | solution.py:269
  (1 shorter events, 0.0 us)
Async XLA Ops:
  0.0 0.8 copy-start

commit v3 on v2

--- a/solution.py
+++ b/solution.py
@@ -8,18 +8,32 @@
 
 HD = 128
 BLOCK = 256
-LISTED = 21
-SHARED = 9
-
-
-def attend_kernel(table, q_ref, kv_ref, o_ref, kbuf, vbuf, sem):
+LATE = 13
+NEARBY = 8
+FACTOR = HD ** (-0.5) * np.log2(np.e)
+NT = (((1,), (1,)), ((), ()))
+
+
+def softmax_terms(scores, values):
+    top = scores[0].max(axis=-1, keepdims=True)
+    for part in scores[1:]:
+        top = jnp.maximum(top, part.max(axis=-1, keepdims=True))
+    total = None
+    for part, value in zip(scores, values):
+        weights = jnp.exp2((part - top) * FACTOR).astype(jnp.bfloat16)
+        term = jnp.dot(weights, value, preferred_element_type=jnp.float32)
+        total = term if total is None else total + term
+    return top, total
+
+
+def last_kernel(table, q_ref, mean_ref, log_ref, kv_ref, o_ref, kbuf, vbuf, sem):
     c = pl.program_id(0)
     slot = c % 2
 
     def copies(step, where):
         made = []
-        for j in range(LISTED):
-            block = table[step * LISTED + j]
+        for j in range(LATE):
+            block = table[step * LATE + j]
             made.append(pltpu.make_async_copy(
                 kv_ref.at[block, :, 0:HD], kbuf.at[where, pl.ds(j * BLOCK, BLOCK)], sem.at[where, 0, j]))
             made.append(pltpu.make_async_copy(
@@ -30,7 +44,7 @@
     def _():
         for copy in copies(0, 0):
             copy.start()
-        vbuf[:, :, HD:2 * HD] = jnp.ones((2, LISTED * BLOCK, HD), jnp.bfloat16)
+        vbuf[:, :, HD:2 * HD] = jnp.ones((2, LATE * BLOCK, HD), jnp.bfloat16)
 
     @pl.when(c + 1 < pl.num_programs(0))
     def _():
@@ -39,20 +53,19 @@
 
     for copy in copies(c, slot):
         copy.wait()
-    factor = HD ** (-0.5) * np.log2(np.e)
     for g in range(4):
-        q = q_ref[:, g * HD:(g + 1) * HD]
-        nt = (((1,), (1,)), ((), ()))
-        lo = SHARED * BLOCK
-        ro = (SHARED + 3 * g) * BLOCK
-        s1 = lax.dot_general(q, kbuf[slot, 0:lo], nt, preferred_element_type=jnp.float32)
-        s2 = lax.dot_general(q, kbuf[slot, ro:ro + 3 * BLOCK], nt, preferred_element_type=jnp.float32)
-        m = jnp.maximum(jnp.max(s1, axis=-1, keepdims=True), jnp.max(s2, axis=-1, keepdims=True))
-        p1 = jnp.exp2((s1 - m) * factor).astype(jnp.bfloat16)
-        p2 = jnp.exp2((s2 - m) * factor).astype(jnp.bfloat16)
-        o = jnp.dot(p1, vbuf[slot, 0:lo], preferred_element_type=jnp.float32)
-        o += jnp.dot(p2, vbuf[slot, ro:ro + 3 * BLOCK], preferred_element_type=jnp.float32)
-        o_ref[:, g * HD:(g + 1) * HD] = (o[:, :HD] / o[:, HD:]).astype(jnp.bfloat16)
+        lanes = slice(g * HD, (g + 1) * HD)
+        q = q_ref[:, lanes]
+        spans = [slice(0, BLOCK), slice((1 + 3 * g) * BLOCK, (4 + 3 * g) * BLOCK)]
+        scores = [lax.dot_general(q, kbuf[slot, span], NT, preferred_element_type=jnp.float32) for span in spans]
+        top, total = softmax_terms(scores, [vbuf[slot, span] for span in spans])
+        early = log_ref[:, lanes]
+        top = top * FACTOR
+        highest = jnp.maximum(early, top)
+        keep = jnp.exp2(early - highest)
+        add = jnp.exp2(top - highest)
+        out = (keep * mean_ref[:, lanes] + add * total[:, :HD]) / (keep + add * total[:, HD:])
+        o_ref[:, lanes] = out.astype(jnp.bfloat16)
 
 
 MESH = pl.DeviceIdType.MESH
@@ -125,7 +138,13 @@
 FIRST = [("z", 1, "B"), ("z", -1, "B"), ("y", 1, "A"), ("y", -1, "A"), ("z", 1, "A"), ("z", -1, "A"), ("y", 1, "B"), ("y", -1, "B")]
 
 
-def gather_kernel(kvh, qh, kv, q, send, recv, send_core, recv_core, send1, recv1, send_own, recv_own, sendx, recvx, local):
+NEEDED = [p for p in FAR if p[1:3] in ((0, 1), (0, -1), (0, 2), (0, -2), (1, 0), (-1, 0), (2, 0))]
+READY = max(FAR.index(p) for p in NEEDED)
+PACE = 6
+
+
+def gather_kernel(kvh, qh, kv, q, mean, log, send, recv, send_core, recv_core, send1, recv1, send_own, recv_own, sendx, recvx, local,
+                  qv, kbuf, vbuf, means, logs, load, store):
     seq = lax.axis_index("seq")
     x = lax.axis_index("head")
     core = lax.rem(seq, 2)
@@ -143,7 +162,7 @@
     for r in (1, 2, 3):
         pl.semaphore_signal(barrier, inc=1, device_id={"seq": seq, "head": lax.rem(x + r, 4)}, device_id_type=MESH)
     own_kv = pltpu.make_async_copy(kvh.at[x], kv.at[seq * 4 + x], local.at[0])
-    own_q = pltpu.make_async_copy(qh.at[x], q.at[x], local.at[1])
+    own_q = pltpu.make_async_copy(qh.at[x], qv.at[x], local.at[1])
     own_kv.start()
     own_q.start()
     pl.semaphore_wait(barrier, 8)
@@ -159,7 +178,7 @@
         return remote(source.at[to], target, sendx.at[which, r], recvx.at[which, r], seq, to)
 
     kv_x = {r: x_copy(kvh, kv.at[seq * 4 + x], 0, r) for r in (1, 3, 2)}
-    q_x = {r: x_copy(qh, q.at[x], 1, r) for r in (1, 3, 2)}
+    q_x = {r: x_copy(qh, qv.at[x], 1, r) for r in (1, 3, 2)}
     for r in (1, 3, 2):
         kv_x[r].start()
 
@@ -209,7 +228,65 @@
             for k in (1, 3, 2):
                 q_x[k].start()
 
-    for piece in FAR:
+    vbuf[:, :, HD:2 * HD] = jnp.ones((4, NEARBY * BLOCK, HD), jnp.bfloat16)
+
+    def flip(i, bit):
+        return i + bit - 2 * bit * lax.rem(i // bit, 2)
+
+    holders = [seq, sibling, (y * NZ + flip(z, 1)) * 2 + core, (y * NZ + flip(z, 2)) * 2 + core,
+               (flip(y, 1) * NZ + z) * 2 + core, (flip(y, 2) * NZ + z) * 2 + core]
+
+    def loads():
+        made = []
+        for c in range(4):
+            blocks = [seq * 4 + c, seq * 4 + (c ^ 1), seq * 4 + (c ^ 2)] + [h * 4 + c for h in holders[1:]]
+            for j, block in enumerate(blocks):
+                made.append(pltpu.make_async_copy(kv.at[block, :, 0:HD], kbuf.at[c, pl.ds(j * BLOCK, BLOCK)], load.at[c, j, 0]))
+                made.append(pltpu.make_async_copy(
+                    kv.at[block, :, HD:2 * HD], vbuf.at[c, pl.ds(j * BLOCK, BLOCK), 0:HD], load.at[c, j, 1]))
+        return made
+
+    def attend(i, _):
+        c = i // 4
+        lanes = pl.ds(pl.multiple_of(lax.rem(i, 4) * HD, HD), HD)
+        scores = lax.dot_general(qv[c, :, lanes], kbuf[c], NT, preferred_element_type=jnp.float32)
+        top, total = softmax_terms([scores], [vbuf[c]])
+        sums = total[:, HD:]
+        means[c, :, lanes] = total[:, :HD] / sums
+        logs[c, :, lanes] = top * FACTOR + jnp.log2(sums)
+        return 0
+
+    def results(c):
+        return [pltpu.make_async_copy(means.at[c], mean.at[c], store.at[0, c]),
+                pltpu.make_async_copy(logs.at[c], log.at[c], store.at[1, c])]
+
+    q_out = pltpu.make_async_copy(qv, q, local.at[2])
+
+    def beside(step):
+        if step == READY:
+            for r in (0, 1, 3, 2):
+                own_copy_in(r).wait_recv()
+            for copy in loads():
+                copy.start()
+            own_q.wait()
+            for r in (1, 3, 2):
+                q_x[r].wait_recv()
+            q_out.start()
+        turn, phase = divmod(step - READY - 3, PACE)
+        if phase == 0 and 0 <= turn < 8:
+            if turn == 0:
+                for copy in loads():
+                    copy.wait()
+            lax.fori_loop(2 * turn, 2 * turn + 2, attend, 0)
+            if turn % 2:
+                for copy in results(turn // 2):
+                    copy.start()
+
+    def own_copy_in(r):
+        block = kv.at[seq * 4 + lax.rem(x + 4 - r, 4)]
+        return remote(block, block, send_own.at[r], recv_own.at[r], sibling, x)
+
+    for step, piece in enumerate(FAR):
         part, oy, oz, half = piece
         if half is None and abs(oy) + abs(oz) == 1:
             axis, way = ("y", -oy) if oy else ("z", -oz)
@@ -226,15 +303,15 @@
         copy = core_copy(piece)
         copy.start()
         everything.append(copy)
-
-    for r in (0, 1, 3, 2):
-        block = kv.at[seq * 4 + lax.rem(x + 4 - r, 4)]
-        remote(block, block, send_own.at[r], recv_own.at[r], sibling, x).wait_recv()
+        beside(step)
+
     for piece in FAR:
         core_copy(piece).wait_recv()
-    own_q.wait()
+    q_out.wait()
+    for c in range(4):
+        for copy in results(c):
+            copy.wait()
     for r in (1, 3, 2):
-        q_x[r].wait_recv()
         q_x[r].wait_send()
         kv_x[r].wait_send()
     for copy in everything:
@@ -244,43 +321,49 @@
 def gather(kvh, qh):
     dma = pltpu.SemaphoreType.DMA
     n = len(FAR)
+    state = jax.ShapeDtypeStruct((4, BLOCK, 4 * HD), jnp.float32)
     return pl.pallas_call(
         gather_kernel,
-        out_shape=(jax.ShapeDtypeStruct((256, BLOCK, 2 * HD), jnp.bfloat16), jax.ShapeDtypeStruct((4, BLOCK, 4 * HD), jnp.bfloat16)),
+        out_shape=(jax.ShapeDtypeStruct((256, BLOCK, 2 * HD), jnp.bfloat16), jax.ShapeDtypeStruct((4, BLOCK, 4 * HD), jnp.bfloat16),
+                   state, state),
         in_specs=[pl.BlockSpec(memory_space=pltpu.VMEM)] * 2,
-        out_specs=[pl.BlockSpec(memory_space=pl.ANY)] * 2,
+        out_specs=[pl.BlockSpec(memory_space=pl.ANY)] * 4,
         scratch_shapes=[dma((n,)), dma((n,)), dma((n,)), dma((n,)), dma((4, 2, 4)), dma((4, 2, 4)), dma((4,)), dma((4,)),
-                        dma((2, 4)), dma((2, 4)), dma((2,))],
+                        dma((2, 4)), dma((2, 4)), dma((3,)),
+                        pltpu.VMEM((4, BLOCK, 4 * HD), jnp.bfloat16),
+                        pltpu.VMEM((4, NEARBY * BLOCK, HD), jnp.bfloat16),
+                        pltpu.VMEM((4, NEARBY * BLOCK, 2 * HD), jnp.bfloat16),
+                        pltpu.VMEM((4, BLOCK, 4 * HD), jnp.float32),
+                        pltpu.VMEM((4, BLOCK, 4 * HD), jnp.float32),
+                        dma((4, NEARBY, 2)), dma((2, 4))],
         compiler_params=pltpu.CompilerParams(collective_id=0, has_side_effects=True),
         name="gather",
     )(kvh, qh)
 
 
 def on_device(queries, key_value, rand_blocks):
-    kv_all, q = gather(key_value.transpose(1, 0, 2), queries.transpose(1, 0, 2))
-    q = q.reshape(1024, 512)
+    kv_all, q, mean, log = gather(key_value.transpose(1, 0, 2), queries.transpose(1, 0, 2))
+    rows = [a.reshape(4 * BLOCK, 4 * HD) for a in (q, mean, log)]
     seq = lax.axis_index("seq")
     head = lax.axis_index("head")
-    blocks = seq * 4 + jnp.arange(4, dtype=jnp.int32)
-    flips = jnp.array([0] + [1 << i for i in range(8)], dtype=jnp.int32)
-    shared = blocks[:, None] ^ flips[None]
+    blocks = ((seq + 8 - 16 * ((seq // 8) % 2)) * 4 + jnp.arange(4, dtype=jnp.int32)).astype(jnp.int32)
     mine = lax.dynamic_slice(rand_blocks, (seq * 4, head * 4, 0), (4, 4, 3)).reshape(4, 12)
-    table = jnp.concatenate([shared, mine], axis=1).reshape(-1).astype(jnp.int32)
+    table = jnp.concatenate([blocks[:, None], mine], axis=1).reshape(-1)
+    rows_of = pl.BlockSpec((BLOCK, 4 * HD), lambda c, t: (c, 0))
     out = pl.pallas_call(
-        attend_kernel,
+        last_kernel,
         grid_spec=pltpu.PrefetchScalarGridSpec(
             num_scalar_prefetch=1, grid=(4,),
-            in_specs=[pl.BlockSpec((BLOCK, 4 * HD), lambda c, t: (c, 0)),
-                      pl.BlockSpec(memory_space=pl.ANY)],
-            out_specs=pl.BlockSpec((BLOCK, 4 * HD), lambda c, t: (c, 0)),
-            scratch_shapes=[pltpu.VMEM((2, LISTED * BLOCK, HD), jnp.bfloat16),
-                            pltpu.VMEM((2, LISTED * BLOCK, 2 * HD), jnp.bfloat16),
-                            pltpu.SemaphoreType.DMA((2, 2, LISTED))]),
-        out_shape=jax.ShapeDtypeStruct((1024, 512), jnp.bfloat16),
+            in_specs=[rows_of, rows_of, rows_of, pl.BlockSpec(memory_space=pl.ANY)],
+            out_specs=rows_of,
+            scratch_shapes=[pltpu.VMEM((2, LATE * BLOCK, HD), jnp.bfloat16),
+                            pltpu.VMEM((2, LATE * BLOCK, 2 * HD), jnp.bfloat16),
+                            pltpu.SemaphoreType.DMA((2, 2, LATE))]),
+        out_shape=jax.ShapeDtypeStruct((4 * BLOCK, 4 * HD), jnp.bfloat16),
         compiler_params=pltpu.CompilerParams(dimension_semantics=("arbitrary",), vmem_limit_bytes=60 << 20),
         name="attend",
-    )(table, q, kv_all)
-    return out.reshape(1024, 1, 512)
+    )(table, *rows, kv_all)
+    return out.reshape(4 * BLOCK, 1, 4 * HD)
 
 
 def solution(mesh):

time: 141 us -> 131 us (0.929)
  Pallas kernels: 134 us -> 124 us
    pallas_call x1, Pallas kernels: 23.7 us -> 11.8 us  [on_device(): pl.pallas_call(last_kernel, grid_spec=pltpu.PrefetchScalarGridSpec(num_sc...]
where the time goes in v3:
time: 131 us; the launch traced here: 130 us
  Pallas kernels  124 us (95%)
  local copies, waits for them, and re-layouts  6.03 us (5%)
    pallas_call x1, Pallas kernels, gather(): pl.pallas_call(gather_kernel, out_shape=(jax.ShapeDtypeStruct((256, BLOCK...  112 us
    pallas_call x1, Pallas kernels, on_device(): pl.pallas_call(last_kernel, grid_spec=pltpu.PrefetchScalarGridSpec(num_sc...  11.8 us
    unnamed x4, local copies, waits for them, and re-layouts  5.07 us

profile of v3, /device:TPU:1, one launch (start us, length us, event | category | flops | bytes accessed | tf_op | source)
XLA Modules:
  0.0 130.2 jit_solution(9268799751749571381)
XLA Ops:
  0.0 0.0 copy-start
  0.0 0.8 copy-done
  0.8 0.1 constant_dynamic-slice_fusion
  0.9 0.1 copy.7
  1.0 0.1 reshape.25
  1.1 0.1 pad_add_fusion
  1.2 0.7 reshape.26.table
  1.8 1.9 %copy.13 = bf16[256,4,256]{2,0,1:T(8,128)(2,1)} copy(bf16[256,4,256]{2,1,0:T(4,128)(2,1)} %param.4) | data formatting | bytes 1048576 | tf_op args[1]
  3.7 2.4 %copy.12 = bf16[256,4,512]{2,0,1:T(8,128)(2,1)} copy(bf16[256,4,512]{2,1,0:T(4,128)(2,1)} %param.3) | data formatting | bytes 2097152 | tf_op args[0]
  6.1 112.1 %gather.1 = (bf16[256,256,256]{2,1,0:T(8,128)(2,1)}, bf16[4,256,512]{2,1,0:T(8,128)(2,1)}, f32[4,256,512]{2,1,0:T(8,128)}, f32[4,256,512]{2,1,0:T(8,128)}) custom-call(bf16[4,256,256]{2,1,0:T(8,128)(2,1)} %bitcast.11, bf16[4,256,512]{2,1,0:T(8,128)(2,1)} %bitcast.10), custom_call_target="tpu_custom_call" | custom-call | tf_op jit(solution)/shard_map/gather/pallas_call | solution.py:325
  118.3 11.8 %attend.1 = bf16[1024,512]{1,0:T(8,128)(2,1)} custom-call(s32[52]{0:T(128)} %reshape.26.table, bf16[1024,512]{1,0:T(8,128)(2,1)} %bitcast.14, f32[1024,512]{1,0:T(8,128)} %bitcast.12, f32[1024,512]{1,0:T(8,128)} %bitcast.13, bf16[256,256,256]{2,1,0:T(8,128)(2,1)} %get-tuple-element.12.kv_ref), custom_call_target="tpu_custom_call" | custom-call | tf_op jit(solution)/shard_map/attend/pallas_call | solution.py:353
  (1 shorter events, 0.0 us)
Async XLA Ops:
  0.0 0.8 copy-start

commit v4 on v3

v4 whole, which is shorter than its diff:
```python
import jax
import jax.numpy as jnp
import numpy as np
from jax import lax
from jax.experimental import pallas as pl
from jax.experimental.pallas import tpu as pltpu
from jax.sharding import PartitionSpec as P

HD = 128
BLOCK = 256
LATE = 12
NEARBY = 9
FACTOR = HD ** (-0.5) * np.log2(np.e)
NT = (((1,), (1,)), ((), ()))


def softmax_terms(scores, values):
    top = scores[0].max(axis=-1, keepdims=True)
    for part in scores[1:]:
        top = jnp.maximum(top, part.max(axis=-1, keepdims=True))
    total = None
    for part, value in zip(scores, values):
        weights = jnp.exp2((part - top) * FACTOR).astype(jnp.bfloat16)
        term = jnp.dot(weights, value, preferred_element_type=jnp.float32)
        total = term if total is None else total + term
    return top, total


def last_kernel(table, q_ref, mean_ref, log_ref, kv_ref, o_ref, kbuf, vbuf, sem):
    c = pl.program_id(0)
    slot = c % 2

    def copies(step, where):
        made = []
        for j in range(LATE):
            block = table[step * LATE + j]
            made.append(pltpu.make_async_copy(
                kv_ref.at[block, :, 0:HD], kbuf.at[where, pl.ds(j * BLOCK, BLOCK)], sem.at[where, 0, j]))
            made.append(pltpu.make_async_copy(
                kv_ref.at[block, :, HD:2 * HD], vbuf.at[where, pl.ds(j * BLOCK, BLOCK), 0:HD], sem.at[where, 1, j]))
        return made

    @pl.when(c == 0)
    def _():
        for copy in copies(0, 0):
            copy.start()
        vbuf[:, :, HD:2 * HD] = jnp.ones((2, LATE * BLOCK, HD), jnp.bfloat16)

    @pl.when(c + 1 < pl.num_programs(0))
    def _():
        for copy in copies(c + 1, 1 - slot):
            copy.start()

    for copy in copies(c, slot):
        copy.wait()
    for g in range(4):
        lanes = slice(g * HD, (g + 1) * HD)
        q = q_ref[:, lanes]
        spans = [slice(3 * g * BLOCK, (3 + 3 * g) * BLOCK)]
        scores = [lax.dot_general(q, kbuf[slot, span], NT, preferred_element_type=jnp.float32) for span in spans]
        top, total = softmax_terms(scores, [vbuf[slot, span] for span in spans])
        early = log_ref[:, lanes]
        top = top * FACTOR
        highest = jnp.maximum(early, top)
        keep = jnp.exp2(early - highest)
        add = jnp.exp2(top - highest)
        out = (keep * mean_ref[:, lanes] + add * total[:, :HD]) / (keep + add * total[:, HD:])
        o_ref[:, lanes] = out.astype(jnp.bfloat16)


MESH = pl.DeviceIdType.MESH
NY = 4
NZ = 8


def forward_rules():
    rules = {}
    todo = [(0, 0, None)]
    while todo:
        piece = todo.pop(0)
        if piece in rules:
            continue
        oy, oz, half = piece
        sends = []
        for way in (1, -1):
            side = 0 if way > 0 else 1
            if oz == 0 and oy == 0:
                sends.append(("z", way, (0, -way, None)))
                sends.append(("y", way, (-way, 0, None)))
            elif oz == 0 and oy == -way:
                sends.append(("y", way, (2, 0, side)))
            elif oz == 0 and oy == 2:
                sends.append(("z", way, (2, -way, half)))
            elif oz * way < 0 and abs(oz) < 3:
                sends.append(("z", way, (oy, oz - way, half)))
            elif oz == -3 * way and oy == 0:
                sends.append(("z", way, (0, 4, side)))
        rules[piece] = sends
        todo += [send[2] for send in sends]
    return rules


def arrival_order(rules):
    free, order, count = {}, [], 1
    events = [(0.0, 0, (0, 0, None))]
    while events:
        events.sort()
        now, _, piece = events.pop(0)
        order.append((piece, now))
        for axis, way, sent in rules[piece]:
            done = max(now, free.get((axis, way), 0.0)) + (BLOCK if sent[2] is None else BLOCK // 2)
            free[axis, way] = done
            events.append((done + 40.0, count, sent))
            count += 1
        if piece[0] == 0:
            for way in (1, -1):
                free["y", way] = max(now, free.get(("y", way), 0.0)) + (BLOCK // 2 if piece[2] is None else BLOCK // 4)
    return order


RULES = forward_rules()
TIMES = arrival_order(RULES)
FAR = [p for p, _ in TIMES if p[:2] != (0, 0)]
SLOT = {p: i for i, p in enumerate(FAR)}
FULL = [p for p in FAR if p[0] in (0, 2)]
NEAR = {("y", 1): 0, ("y", -1): 1, ("z", 1): 2, ("z", -1): 3}
OFFSETS = (0, 1, -1, 2, -2, 3, -3, 4)
PICKS = [(oz, step, other) for oz in OFFSETS for step in ((1, -1, 2) if oz == 4 else (1, -1)) for other in (1, 0)
         if (oz, other) != (0, 0)]
NEEDED = [p for p in FAR if p[:2] in ((0, 1), (0, -1), (0, 2), (0, -2), (0, 4), (1, 0), (-1, 0), (2, 0))]
READY = max(FAR.index(p) for p in NEEDED)


def gather_kernel(want, kvh, qh, kv, q, mean, log, send, recv, send_core, recv_core, send1, recv1, send_own, recv_own, sendx, recvx, local,
                  qv, kbuf, vbuf, means, logs, load, store, stage, send_pick, recv_pick, take, *held):
    seq = lax.axis_index("seq")
    x = lax.axis_index("head")
    core = lax.rem(seq, 2)
    z = lax.rem(seq // 2, NZ)
    y = seq // (2 * NZ)

    def at(oy, oz, c):
        return (lax.rem(y + (oy + NY), NY) * NZ + lax.rem(z + (oz + NZ), NZ)) * 2 + c

    where = {("y", 1): at(1, 0, core), ("y", -1): at(-1, 0, core), ("z", 1): at(0, 1, core), ("z", -1): at(0, -1, core)}
    sibling = at(0, 0, 1 - core)
    barrier = pltpu.get_barrier_semaphore()
    others = list(where.values()) + [sibling, at(2, 0, core)] + [at(oy, 0, 1 - core) for oy in (1, -1, 2)]
    for target in others:
        pl.semaphore_signal(barrier, inc=1, device_id={"seq": target, "head": x}, device_id_type=MESH)
    for r in (1, 2, 3):
        pl.semaphore_signal(barrier, inc=1, device_id={"seq": seq, "head": lax.rem(x + r, 4)}, device_id_type=MESH)
    own_kv = pltpu.make_async_copy(kvh.at[x], kv.at[seq * 4 + x], local.at[0])
    own_q = pltpu.make_async_copy(qh.at[x], qv.at[x], local.at[1])
    own_kv.start()
    own_q.start()
    pl.semaphore_wait(barrier, len(others) + 3)

    def remote(src, dst, s, r, target, head):
        return pltpu.make_async_remote_copy(src_ref=src, dst_ref=dst, send_sem=s, recv_sem=r,
                                            device_id={"seq": target, "head": head}, device_id_type=MESH)

    everything = []

    def begin(copy):
        copy.start()
        everything.append(copy)

    def x_copy(source, target, which, r):
        to = lax.rem(x + r, 4)
        return remote(source.at[to], target, sendx.at[which, r], recvx.at[which, r], seq, to)

    kv_x = {r: x_copy(kvh, kv.at[seq * 4 + x], 0, r) for r in (1, 3, 2)}
    q_x = {r: x_copy(qh, qv.at[x], 1, r) for r in (1, 3, 2)}
    for r in (1, 3, 2):
        kv_x[r].start()

    def own_block(r):
        return kv.at[seq * 4 + lax.rem(x + 4 - r, 4)]

    def first_copy(axis, way, r):
        block = own_block(r)
        i = NEAR[axis, way]
        return remote(block, block, send1.at[i, r], recv1.at[i, r], where[axis, way], x)

    def own_copy(r):
        block = own_block(r)
        return remote(block, block, send_own.at[r], recv_own.at[r], sibling, x)

    def piece_ref(oy, oz, half, c):
        start, count = (0, 4) if half is None else (2 * half, 2)
        return kv.at[pl.ds(at(oy, oz, c) * 4 + start, count)]

    def far_copy(oy, oz, axis, way, sent):
        ref = piece_ref(oy, oz, sent[2], core)
        i = SLOT[sent]
        return remote(ref, ref, send.at[i], recv.at[i], where[axis, way], x)

    def core_copy(piece):
        ref = piece_ref(*piece, core)
        i = SLOT[piece]
        return remote(ref, ref, send_core.at[i], recv_core.at[i], sibling, x)

    def pick_copy(i):
        oz, step, other = PICKS[i]
        reader = at(step, 0, 1 - core if other else core)
        return remote(stage.at[i], kv.at[at(0, oz, core) * 4], send_pick.at[i], recv_pick.at[i], reader, x)

    def pick(oz):
        i = OFFSETS.index(oz)
        copy = pltpu.make_async_copy(piece_ref(0, oz, None, core), held[i], take.at[i])
        copy.start()
        copy.wait()
        mine = [j for j in range(len(PICKS)) if PICKS[j][0] == oz]
        for j in mine:
            _, step, other = PICKS[j]
            reader_core = 1 - core if other else core
            block = want[({1: 0, -1: 16, 2: 32}[step] + i) + reader_core * 8]
            stage[j] = held[i][block]
        for j in mine:
            begin(pick_copy(j))

    vbuf[:, :, HD:2 * HD] = jnp.ones((4, NEARBY * BLOCK, HD), jnp.bfloat16)

    def flip(i, bit):
        return i + bit - 2 * bit * lax.rem(i // bit, 2)

    holders = [seq, sibling, (y * NZ + flip(z, 1)) * 2 + core, (y * NZ + flip(z, 2)) * 2 + core, (y * NZ + flip(z, 4)) * 2 + core,
               (flip(y, 1) * NZ + z) * 2 + core, (flip(y, 2) * NZ + z) * 2 + core]

    def loads():
        made = []
        for c in range(4):
            blocks = [seq * 4 + c, seq * 4 + (c ^ 1), seq * 4 + (c ^ 2)] + [h * 4 + c for h in holders[1:]]
            for j, block in enumerate(blocks):
                made.append(pltpu.make_async_copy(kv.at[block, :, 0:HD], kbuf.at[c, pl.ds(j * BLOCK, BLOCK)], load.at[c, j, 0]))
                made.append(pltpu.make_async_copy(
                    kv.at[block, :, HD:2 * HD], vbuf.at[c, pl.ds(j * BLOCK, BLOCK), 0:HD], load.at[c, j, 1]))
        return made

    def attend(i, _):
        c = i // 4
        lanes = pl.ds(pl.multiple_of(lax.rem(i, 4) * HD, HD), HD)
        scores = lax.dot_general(qv[c, :, lanes], kbuf[c], NT, preferred_element_type=jnp.float32)
        top, total = softmax_terms([scores], [vbuf[c]])
        sums = total[:, HD:]
        means[c, :, lanes] = total[:, :HD] / sums
        logs[c, :, lanes] = top * FACTOR + jnp.log2(sums)
        return 0

    def results(c):
        return [pltpu.make_async_copy(means.at[c], mean.at[c], store.at[0, c]),
                pltpu.make_async_copy(logs.at[c], log.at[c], store.at[1, c])]

    q_out = pltpu.make_async_copy(qv, q, local.at[2])

    def turn(i):
        if i == 0:
            for copy in loads():
                copy.wait()
        lax.fori_loop(2 * i, 2 * i + 2, attend, 0)
        if i % 2:
            for copy in results(i // 2):
                copy.start()

    for r in (0, 1, 3, 2):
        if r == 0:
            own_kv.wait()
        else:
            kv_x[r].wait_recv()
        for axis, way in (("z", 1), ("z", -1), ("y", 1), ("y", -1)):
            begin(first_copy(axis, way, r))
        begin(own_copy(r))
        if r == 0:
            for k in (1, 3, 2):
                q_x[k].start()
    pick(0)

    turns = 0
    for step, piece in enumerate(FAR):
        oy, oz, half = piece
        if half is None and abs(oy) + abs(oz) == 1:
            axis, way = ("y", -oy) if oy else ("z", -oz)
            for r in (0, 1, 3, 2):
                first_copy(axis, way, r).wait_recv()
        else:
            ref = piece_ref(oy, oz, half, core)
            i = SLOT[piece]
            remote(ref, ref, send.at[i], recv.at[i], sibling, x).wait_recv()
        for axis, way, sent in RULES[piece]:
            begin(far_copy(oy, oz, axis, way, sent))
        if piece in FULL:
            begin(core_copy(piece))
        if oy == 0 and (half is None or all(p in FAR[:step + 1] for p in ((0, 4, 0), (0, 4, 1)))):
            pick(oz)
        if step == READY:
            for r in (0, 1, 3, 2):
                own_copy(r).wait_recv()
            for copy in loads():
                copy.start()
            own_q.wait()
            for r in (1, 3, 2):
                q_x[r].wait_recv()
            q_out.start()
        elif step > READY and turns < 8:
            turn(turns)
            turns += 1
    for i in range(turns, 8):
        turn(i)

    for i, (oz, step, other) in enumerate(PICKS):
        ref = kv.at[at(-step, oz, 1 - core if other else core) * 4]
        remote(stage.at[i], ref, send_pick.at[i], recv_pick.at[i], sibling, x).wait_recv()
    for piece in FULL:
        core_copy(piece).wait_recv()
    q_out.wait()
    for c in range(4):
        for copy in results(c):
            copy.wait()
    for r in (1, 3, 2):
        q_x[r].wait_send()
        kv_x[r].wait_send()
    for copy in everything:
        copy.wait_send()


def gather(want, kvh, qh):
    dma = pltpu.SemaphoreType.DMA
    n = len(FAR)
    state = jax.ShapeDtypeStruct((4, BLOCK, 4 * HD), jnp.float32)
    return pl.pallas_call(
        gather_kernel,
        out_shape=(jax.ShapeDtypeStruct((256, BLOCK, 2 * HD), jnp.bfloat16), jax.ShapeDtypeStruct((4, BLOCK, 4 * HD), jnp.bfloat16),
                   state, state),
        in_specs=[pl.BlockSpec(memory_space=pltpu.SMEM)] + [pl.BlockSpec(memory_space=pltpu.VMEM)] * 2,
        out_specs=[pl.BlockSpec(memory_space=pl.ANY)] * 4,
        scratch_shapes=[dma((n,)), dma((n,)), dma((n,)), dma((n,)), dma((4, 4)), dma((4, 4)), dma((4,)), dma((4,)),
                        dma((2, 4)), dma((2, 4)), dma((3,)),
                        pltpu.VMEM((4, BLOCK, 4 * HD), jnp.bfloat16),
                        pltpu.VMEM((4, NEARBY * BLOCK, HD), jnp.bfloat16),
                        pltpu.VMEM((4, NEARBY * BLOCK, 2 * HD), jnp.bfloat16),
                        pltpu.VMEM((4, BLOCK, 4 * HD), jnp.float32),
                        pltpu.VMEM((4, BLOCK, 4 * HD), jnp.float32),
                        dma((4, NEARBY, 2)), dma((2, 4)),
                        pltpu.VMEM((len(PICKS), BLOCK, 2 * HD), jnp.bfloat16), dma((len(PICKS),)), dma((len(PICKS),)), dma((8,))]
        + [pltpu.VMEM((4, BLOCK, 2 * HD), jnp.bfloat16) for _ in OFFSETS],
        compiler_params=pltpu.CompilerParams(collective_id=0, has_side_effects=True),
        name="gather",
    )(want, kvh, qh)


def on_device(queries, key_value, rand_blocks):
    seq = lax.axis_index("seq")
    head = lax.axis_index("head")
    core, z, y = seq % 2, seq // 2 % NZ, seq // (2 * NZ)

    def lists(first, count):
        return lax.dynamic_slice(rand_blocks, (first * 4, head * 4, 0), (count * 4, 4, 3))

    asked = jnp.stack([lists((y + step) % NY * (2 * NZ) + z * 2, 2) for step in (1, 3, 2)]).reshape(3, 2, 1, 48)
    origins = ((y * NZ + (z + np.array(OFFSETS, np.int32) + NZ) % NZ) * 2 + core)[None, None, :, None]
    want = jnp.sum(jnp.where(asked // 4 == origins, asked % 4, 0), axis=-1, dtype=jnp.int32).reshape(-1)
    kv_all, q, mean, log = gather(want, key_value.transpose(1, 0, 2), queries.transpose(1, 0, 2))
    rows = [a.reshape(4 * BLOCK, 4 * HD) for a in (q, mean, log)]
    listed = lists(seq, 1).reshape(48)
    holder = listed // 4
    from_y, from_z = (holder // (2 * NZ) + NY - y) % NY, (holder // 2 % NZ + NZ - z) % NZ
    whole = jnp.where(from_y % 2 == 0, ~((from_y == 2) & (from_z == 4)), (from_z == 0) & (holder % 2 == core))
    table = jnp.where(whole, listed, holder * 4).astype(jnp.int32)
    rows_of = pl.BlockSpec((BLOCK, 4 * HD), lambda c, t: (c, 0))
    out = pl.pallas_call(
        last_kernel,
        grid_spec=pltpu.PrefetchScalarGridSpec(
            num_scalar_prefetch=1, grid=(4,),
            in_specs=[rows_of, rows_of, rows_of, pl.BlockSpec(memory_space=pl.ANY)],
            out_specs=rows_of,
            scratch_shapes=[pltpu.VMEM((2, LATE * BLOCK, HD), jnp.bfloat16),
                            pltpu.VMEM((2, LATE * BLOCK, 2 * HD), jnp.bfloat16),
                            pltpu.SemaphoreType.DMA((2, 2, LATE))]),
        out_shape=jax.ShapeDtypeStruct((4 * BLOCK, 4 * HD), jnp.bfloat16),
        compiler_params=pltpu.CompilerParams(dimension_semantics=("arbitrary",), vmem_limit_bytes=60 << 20),
        name="attend",
    )(table, *rows, kv_all)
    return out.reshape(4 * BLOCK, 1, 4 * HD)


def solution(mesh):
    in_specs = (P(("seq", "head"), None, None), P(("seq", "head"), None, None), P())
    return jax.shard_map(on_device, mesh=mesh, in_specs=in_specs, out_specs=P("seq", "head", None), check_vma=False)
```

time: 131 us -> 125 us (0.954)
  Pallas kernels: 124 us -> 115 us
  other arithmetic: 0.08 us -> 1.65 us
    pallas_call x1, Pallas kernels: 112 us -> 105 us  [gather(): pl.pallas_call(gather_kernel, out_shape=(jax.ShapeDtypeStruct((256, BLOCK...]
    unnamed x4 -> x6, local copies, waits for them, and re-layouts: 5.07 us -> 3.07 us
    dynamic_slice x2 -> x6, local copies, waits for them, and re-layouts: 0.19 us -> 2.07 us  [lists(): lax.dynamic_slice(rand_blocks, (first * 4, head * 4, 0), (count * 4, 4, 3))]
where the time goes in v4:
time: 125 us; the launch traced here: 124 us
  Pallas kernels  115 us (92%)
  local copies, waits for them, and re-layouts  6.19 us (5%)
  other arithmetic  1.65 us (1%)
    pallas_call x1, Pallas kernels, gather(): pl.pallas_call(gather_kernel, out_shape=(jax.ShapeDtypeStruct((256, BLOCK...  105 us
    pallas_call x1, Pallas kernels, on_device(): pl.pallas_call(last_kernel, grid_spec=pltpu.PrefetchScalarGridSpec(num_sc...  10.6 us
    unnamed x6, local copies, waits for them, and re-layouts  3.07 us

profile of v4, /device:TPU:1, one launch (start us, length us, event | category | flops | bytes accessed | tf_op | source)
XLA Modules:
  0.0 123.5 jit_solution(3586136356529463216)
XLA Ops:
  0.0 0.0 copy-start
  0.0 0.8 fusion.4
  0.8 0.8 constant_dynamic-slice_fusion.3
  1.5 0.1 copy.17
  1.7 0.1 reshape.300
  1.8 0.6 select_select_fusion.table
  2.4 0.9 constant_dynamic-slice_fusion
  3.2 0.1 copy.20
  3.4 0.1 stack.14
  3.5 0.1 copy.18
  3.6 0.1 stack.12
  3.7 0.1 copy.19
  3.8 0.1 stack.13
  3.9 0.2 select_reduce_fusion
  4.2 0.7 reshape.301.want
  4.8 1.9 %copy.26 = bf16[256,4,256]{2,0,1:T(8,128)(2,1)} copy(bf16[256,4,256]{2,1,0:T(4,128)(2,1)} %param.5) | data formatting | bytes 1048576 | tf_op args[1]
  6.7 0.0 copy-done
  6.7 1.2 copy.25
  7.9 104.9 %gather.1 = (bf16[256,256,256]{2,1,0:T(8,128)(2,1)}, bf16[4,256,512]{2,1,0:T(8,128)(2,1)}, f32[4,256,512]{2,1,0:T(8,128)}, f32[4,256,512]{2,1,0:T(8,128)}) custom-call(s32[48]{0:T(128)} %reshape.301.want, bf16[4,256,256]{2,1,0:T(8,128)(2,1)} %bitcast.11, bf16[4,256,512]{2,1,0:T(8,128)(2,1)} %bitcast.10), custom_call_target="tpu_custom_call" | custom-call | tf_op jit(solution)/shard_map/gather/pallas_call | solution.py:331
  112.8 10.6 %attend.1 = bf16[1024,512]{1,0:T(8,128)(2,1)} custom-call(s32[48]{0:T(128)} %select_select_fusion.table, bf16[1024,512]{1,0:T(8,128)(2,1)} %bitcast.14, f32[1024,512]{1,0:T(8,128)} %bitcast.12, f32[1024,512]{1,0:T(8,128)} %bitcast.13, bf16[256,256,256]{2,1,0:T(8,128)(2,1)} %get-tuple-element.12.kv_ref), custom_call_target="tpu_custom_call" | custom-call | tf_op jit(solution)/shard_map/attend/pallas_call | solution.py:371
  (4 shorter events, 0.0 us)
Async XLA Ops:
  0.0 6.7 %copy-start = (bf16[256,4,512]{2,1,0:T(4,128)(2,1)S(1)}, bf16[256,4,512]{2,1,0:T(4,128)(2,1)}, u32[]{:S(2)}) copy-start(bf16[256,4,512]{2,1,0:T(4,128)(2,1)} %param.4) | copy-start | bytes 3145732
